TPU v7x, 32 devices: a whole 2x2x4 slice. The times are simulated.
32 devices in a mesh: owner: 4 (over z), rows: 8 (over y, x, core).
Axes of the slice: x: 2, y: 2, z: 4, core: 2. Of those that a mesh axis runs over, the one named last changes fastest.
Arguments:
- w_gate: float32 [128, 2048, 768], P('owner', 'rows'), may hold values from -0.1875 to 0.1875
- w_up: float32 [128, 2048, 768], P('owner', 'rows'), may hold values from -0.1875 to 0.1875
- router_weight: float32 [2048, 128], P('rows', 'owner'), may hold values from -0.125 to 0.125
- router_gain: float32 [2048], P('rows'), may hold values from 0.25 to 1.75
Outputs:
- serve_gate: bfloat16 [128, 2048, 768], P('owner', None, 'rows')
- serve_up: bfloat16 [128, 2048, 768], P('owner', None, 'rows')
- scale_gate: float32 [128, 768], P('owner', 'rows')
- scale_up: float32 [128, 768], P('owner', 'rows')
- serve_router: bfloat16 [2048, 128], replicated
All inputs are finite; a program needn't handle non-finite values. Where the computation divides by a largest or mean magnitude, that divisor is 1e-20 or more.
Results may differ from a plain program's by a relative error of at most 0.001.
Values may be sent and summed in bfloat16 or wider, within the bound.
A program may use at most 192 MiB of HBM per device.

v0:
```python
import jax
import jax.numpy as jnp
from jax import lax
from jax.sharding import PartitionSpec as P

D_MODEL = 2048


def on_device(w_gate, w_up, router_weight, router_gain):
    total_gate, total_up = lax.psum(
        (jnp.sum(jnp.abs(w_gate), axis=1), jnp.sum(jnp.abs(w_up), axis=1)), "rows"
    )
    scale_gate = total_gate / D_MODEL
    scale_up = total_up / D_MODEL
    narrow_gate, narrow_up = (
        (w_gate / jnp.expand_dims(scale_gate, 1)).astype(jnp.bfloat16),
        (w_up / jnp.expand_dims(scale_up, 1)).astype(jnp.bfloat16),
    )
    serve_gate, serve_up = (
        lax.all_to_all(narrow_gate, "rows", split_axis=2, concat_axis=1, tiled=True),
        lax.all_to_all(narrow_up, "rows", split_axis=2, concat_axis=1, tiled=True),
    )
    scale_gate = lax.dynamic_slice_in_dim(
        scale_gate, lax.axis_index("rows") * serve_gate.shape[2], serve_gate.shape[2], axis=1
    )
    scale_up = lax.dynamic_slice_in_dim(
        scale_up, lax.axis_index("rows") * serve_up.shape[2], serve_up.shape[2], axis=1
    )
    part_router = (router_weight * router_gain[:, None]).astype(jnp.bfloat16)
    row_router = lax.all_gather(part_router, "rows", axis=0, tiled=True)
    serve_router = lax.all_gather(row_router, "owner", axis=1, tiled=True)
    return (serve_gate, serve_up, scale_gate, scale_up, serve_router)


def solution(mesh):
    placed = (P("owner", "rows", None), P("owner", "rows", None), P("rows", "owner"), P("rows"))
    return jax.shard_map(
        on_device,
        mesh=mesh,
        in_specs=placed,
        out_specs=(
            P("owner", None, "rows"),
            P("owner", None, "rows"),
            P("owner", "rows"),
            P("owner", "rows"),
            P(),
        ),
        check_vma=False,
    )
```

profile of v0, /device:TPU:0, one launch (start us, length us, event | category | flops | bytes accessed | tf_op | source)
XLA Modules:
  0.0 481.1 jit_solution(11326135817132377053)
XLA Ops:
  7.2 0.0 all-reduce.3.cloned.1.call-start
  7.2 17.4 %abs_reduce_fusion = (f32[32,768]{1,0:T(8,128)}, f32[32,768]{1,0:T(8,128)}) fusion(f32[32,256,768]{2,1,0:T(8,128)} %param.5, f32[32,256,768]{2,1,0:T(8,128)} %param.4), kind=kLoop, calls=%fused_computation.1 | loop fusion | flops 25116672 | bytes 50528256 | tf_op jit(solution)/shard_map/reduce_sum | solution.py:11
  24.6 0.0 all-reduce.3.cloned.1.call-update
  24.7 25.1 %copy.25 = f32[32,256,768]{1,0,2:T(8,128)} copy(f32[32,256,768]{2,1,0:T(8,128)} %param.5) | data formatting | bytes 50331648 | tf_op args[1]
  49.8 31.5 %all-reduce.3.cloned.1.call-done = (f32[32,768]{1,0:T(8,128)}, f32[32,768]{1,0:T(8,128)}) async-done(((f32[32,768]{1,0:T(8,128)}, f32[32,768]{1,0:T(8,128)}), (f32[32,768]{1,0:T(8,128)}, f32[32,768]{1,0:T(8,128)})) %all-reduce.3.cloned.1.call-update) | async-done | bytes 196624 | tf_op jit(solution)/shard_map/psum | solution.py:10
  81.3 0.9 broadcast_multiply_fusion
  82.2 0.2 copy.24
  82.4 14.1 %divide_convert_fusion = bf16[32,256,768]{1,0,2:T(8,128)(2,1)} fusion(f32[32,256,768]{1,0,2:T(8,128)} %copy.25, f32[32,768]{0,1:T(8,128)S(1)} %copy.24), kind=kLoop, calls=%fused_computation | loop fusion | flops 12582912 | bytes 37847040 | tf_op jit(solution)/shard_map/convert_element_type | solution.py:17
  96.5 5.4 %all-to-all-start.1 = ((bf16[32,256,768]{1,0,2:T(8,128)(2,1)}), bf16[32,256,768]{1,0,2:T(8,128)(2,1)}, u32[]{:S(2)}, u32[]{:S(2)}) async-start(bf16[32,256,768]{1,0,2:T(8,128)(2,1)} %divide_convert_fusion), calls=%async_computation.1 | async-start | bytes 25165824 | tf_op jit(solution)/shard_map/all_to_all | solution.py:21
  101.9 0.0 copy-start
  101.9 25.1 %copy.21 = f32[32,256,768]{1,0,2:T(8,128)} copy(f32[32,256,768]{2,1,0:T(8,128)} %param.4) | data formatting | bytes 50331648 | tf_op args[0]
  127.1 0.0 copy-done
  127.1 0.2 copy.20
  127.2 0.0 copy-start.1
  127.3 0.0 copy-start.2
  127.3 14.1 %divide_convert_fusion.1 = bf16[32,256,768]{1,0,2:T(8,128)(2,1)} fusion(f32[32,256,768]{1,0,2:T(8,128)} %copy.21, f32[32,768]{0,1:T(8,128)S(1)} %copy.20), kind=kLoop, calls=%fused_computation.2 | loop fusion | flops 12582912 | bytes 37847040 | tf_op jit(solution)/shard_map/convert_element_type | solution.py:16
  141.4 99.5 %all-to-all-done.1 = bf16[32,256,768]{1,0,2:T(8,128)(2,1)} async-done(((bf16[32,256,768]{1,0,2:T(8,128)(2,1)}), bf16[32,256,768]{1,0,2:T(8,128)(2,1)}, u32[]{:S(2)}, u32[]{:S(2)}) %all-to-all-start.1) | async-done | bytes 12582944 | tf_op jit(solution)/shard_map/all_to_all | solution.py:21
  240.9 5.4 %all-to-all-start = ((bf16[32,256,768]{1,0,2:T(8,128)(2,1)}), bf16[32,256,768]{1,0,2:T(8,128)(2,1)}, u32[]{:S(2)}, u32[]{:S(2)}) async-start(bf16[32,256,768]{1,0,2:T(8,128)(2,1)} %divide_convert_fusion.1), calls=%async_computation | async-start | bytes 25165824 | tf_op jit(solution)/shard_map/all_to_all | solution.py:20
  246.3 0.0 copy-done.1
  246.3 0.0 copy-done.2
  246.3 142.4 %all_gather.6 = bf16[2048,32]{0,1:T(8,128)(2,1)S(1)} all-gather(bf16[256,32]{0,1:T(8,128)(2,1)S(1)} %multiply_convert_fusion), channel_id=1, replica_groups=mesh['owner'=4,'rows'=8] {'rows'}, dimensions={0}, use_global_device_ids=true | all-gather | bytes 147456 | tf_op jit(solution)/shard_map/all_gather | solution.py:30
  388.8 16.1 %all_gather.7 = bf16[2048,128]{0,1:T(8,128)(2,1)S(1)} all-gather(bf16[2048,32]{0,1:T(8,128)(2,1)S(1)} %all_gather.6), channel_id=1, replica_groups=mesh['owner'=4,'rows'=8] {'owner'}, dimensions={1}, use_global_device_ids=true | all-gather | bytes 655360 | tf_op jit(solution)/shard_map/all_gather | solution.py:31
  404.8 1.0 copy.28
  405.8 0.7 constant_dynamic-slice_fusion
  406.5 0.7 constant_dynamic-slice_fusion.1
  407.2 14.1 %copy.27 = bf16[32,8,256,96]{2,1,3,0:T(8,128)(2,1)} copy(bf16[32,8,256,96]{2,0,3,1:T(8,128)(2,1)} %bitcast.5) | data formatting | bytes 25165824 | tf_op jit(solution)/shard_map/all_to_all | solution.py:21
  421.2 19.5 %all_to_all.33 = bf16[32,2048,96]{1,2,0:T(8,128)(2,1)} reshape(bf16[32,8,256,96]{2,1,3,0:T(8,128)(2,1)} %copy.27) | data formatting | bytes 25165824 | tf_op jit(solution)/shard_map/all_to_all | solution.py:21
  440.7 0.0 all-to-all-done
  440.7 14.1 %copy.23 = bf16[32,8,256,96]{2,1,3,0:T(8,128)(2,1)} copy(bf16[32,8,256,96]{2,0,3,1:T(8,128)(2,1)} %bitcast.2) | data formatting | bytes 25165824 | tf_op jit(solution)/shard_map/all_to_all | solution.py:20
  454.8 19.5 %all_to_all.29 = bf16[32,2048,96]{1,2,0:T(8,128)(2,1)} reshape(bf16[32,8,256,96]{2,1,3,0:T(8,128)(2,1)} %copy.23) | data formatting | bytes 25165824 | tf_op jit(solution)/shard_map/all_to_all | solution.py:20
  (2 shorter events, 0.0 us)
Async XLA Ops:
  7.2 74.2 %all-reduce.3.cloned.1.call-start = ((), (), s32[]{:S(2)}) async-start(), calls=%async_computation.2 | async-start | bytes 393216 | tf_op jit(solution)/shard_map/psum | solution.py:10
  96.5 144.4 %all-to-all-start.1 = ((bf16[32,256,768]{1,0,2:T(8,128)(2,1)}), bf16[32,256,768]{1,0,2:T(8,128)(2,1)}, u32[]{:S(2)}, u32[]{:S(2)}) async-start(bf16[32,256,768]{1,0,2:T(8,128)(2,1)} %divide_convert_fusion), calls=%async_computation.1 | async-start | bytes 25165824 | tf_op jit(solution)/shard_map/all_to_all | solution.py:21
  101.9 25.1 %copy-start = (f32[32,768]{1,0:T(8,128)S(1)}, f32[32,768]{1,0:T(8,128)}, u32[]{:S(2)}) copy-start(f32[32,768]{1,0:T(8,128)} %get-tuple-element.10) | copy-start | bytes 294916
  127.2 119.0 %copy-start.1 = (f32[256,32]{0,1:T(8,128)S(1)}, f32[256,32]{0,1:T(8,128)}, u32[]{:S(2)}) copy-start(f32[256,32]{0,1:T(8,128)} %param.6) | copy-start | bytes 98308
  127.3 119.0 %copy-start.2 = (f32[256]{0:T(256)S(1)}, f32[256]{0:T(256)}, u32[]{:S(2)}) copy-start(f32[256]{0:T(256)} %param.7) | copy-start | bytes 3076
  240.9 199.8 %all-to-all-start = ((bf16[32,256,768]{1,0,2:T(8,128)(2,1)}), bf16[32,256,768]{1,0,2:T(8,128)(2,1)}, u32[]{:S(2)}, u32[]{:S(2)}) async-start(bf16[32,256,768]{1,0,2:T(8,128)(2,1)} %divide_convert_fusion.1), calls=%async_computation | async-start | bytes 25165824 | tf_op jit(solution)/shard_map/all_to_all | solution.py:20
Sparse Core Ops, SparseCore 0:
  24.8 56.4 all-reduce.2
where the time goes:
time: 483 us; the launch traced here: 481 us
  blocking collectives  158 us (33%)
  waiting for transfers between devices  131 us (27%)
  local copies, waits for them, and re-layouts  120 us (25%)
  other arithmetic  46.6 us (10%)
  between operations  14.1 us (3%)
  starting transfers between devices  10.8 us (2%)
    all_gather x1, blocking collectives, on_device(): row_router = lax.all_gather(part_router, 'rows', axis=0, tiled=True)  142 us
    all_to_all x1, waiting for transfers between devices, on_device(): lax.all_to_all(narrow_up, 'rows', split_axis=2, concat_axis=1, tiled=True)  99.5 us
    unnamed x9, local copies, waits for them, and re-layouts  51.3 us
    all_to_all x2, local copies, waits for them, and re-layouts, on_device(): lax.all_to_all(narrow_gate, 'rows', split_axis=2, concat_axis=1, tiled=True)  33.6 us
    all_to_all x2, local copies, waits for them, and re-layouts, on_device(): lax.all_to_all(narrow_up, 'rows', split_axis=2, concat_axis=1, tiled=True)  33.6 us
    psum x1, waiting for transfers between devices, on_device(): lax.psum((jnp.sum(jnp.abs(w_gate), axis=1), jnp.sum(jnp.abs(w_up), axis=1...  31.5 us
    reduce_sum x1, other arithmetic, on_device(): jnp.sum(jnp.abs(w_up), axis=1)  17.4 us
    all_gather x1, blocking collectives, on_device(): serve_router = lax.all_gather(row_router, 'owner', axis=1, tiled=True)  16.1 us
  transfers between devices with their start and end apart: 3, of which 2 were waited for; matrix products, arithmetic and copies ran while one was open for 17% of the time, Pallas kernels for 0%

commit v1 on v0

v1 whole, which is shorter than its diff:
```python
import functools

import jax
import jax.numpy as jnp
from jax import lax
from jax.experimental import pallas as pl
from jax.experimental.pallas import tpu as pltpu
from jax.sharding import PartitionSpec as P

MESH = pl.DeviceIdType.MESH
WINDOW = 6
LOADS = 3
PAIR_LAG = 2
LAG = 4
HELD = LOADS + LAG
SUMS = 2 * LAG + 2


def peer_steps(n):
    far = list(range(2, n, 2))
    return far + [k + 1 for k in far] + [1]


def toggled(index, k):
    result, bit = index, 1
    while bit <= k:
        if k & bit:
            result = result + bit * (1 - 2 * lax.rem(index // bit, 2))
        bit *= 2
    return result


def exchange(
    experts, n, owners, depth,
    gate, up, router, gain,
    pieces, routed, scales,
    window, stage, row_block, part, partner, both, others,
    load_sem, send_sem, recv_sem, self_sem, pair_send, pair_recv, sum_send, sum_recv,
    own_sem, z_send, z_recv, r_send, r_recv,
):
    me, mine = lax.axis_index("rows"), lax.axis_index("owner")
    units, piece, width = 2 * experts, pieces.shape[2], gate.shape[2]
    peers = [toggled(me, k) for k in peer_steps(n)]
    alike = [toggled(me, k) for k in range(2, n, 2)]
    columns = [lax.rem(mine + k, owners) for k in range(1, owners)]

    barrier = pltpu.get_barrier_semaphore()
    for p in peers:
        pl.semaphore_signal(barrier, inc=1, device_id=(mine, p), device_id_type=MESH)
    for c in columns:
        pl.semaphore_signal(barrier, inc=1, device_id=(c, me), device_id_type=MESH)

    def load(s, go):
        for matrix, first in ((gate, 0), (up, experts)):
            @pl.when((s >= first) & (s < first + experts))
            def _():
                slot = lax.rem(s, HELD)
                copy = pltpu.make_async_copy(matrix.at[s - first], window.at[slot], load_sem.at[slot])
                copy.start() if go else copy.wait()

    def pair(s):
        slot = lax.rem(s, SUMS)
        return pltpu.make_async_remote_copy(
            part.at[s], partner.at[s], pair_send.at[slot], pair_recv.at[slot],
            device_id=(mine, toggled(me, 1)), device_id_type=MESH,
        )

    def chips(s):
        slot = lax.rem(s, SUMS)
        return [
            pltpu.make_async_remote_copy(
                both.at[s], others.at[s, i], sum_send.at[slot, i], sum_recv.at[slot, i],
                device_id=(mine, p), device_id_type=MESH,
            )
            for i, p in enumerate(alike)
        ]

    def parts(s):
        slot, land = lax.rem(s, WINDOW), lax.rem(s, 2 * WINDOW)

        def cut(p):
            return stage.at[slot, pl.ds(pl.multiple_of(p * piece, piece), piece)]

        far = [
            pltpu.make_async_remote_copy(
                cut(p), pieces.at[s, me], send_sem.at[slot, i], recv_sem.at[land, i],
                device_id=(mine, p), device_id_type=MESH,
            )
            for i, p in enumerate(peers)
        ]
        return far, pltpu.make_async_copy(cut(me), pieces.at[s, me], self_sem.at[slot])

    def send(s):
        far, near = parts(s)
        for copy in far:
            copy.start()
        near.start()

    def settle(s):
        far, near = parts(s)
        for copy in far:
            copy.wait()
        near.wait()

    def summed(s):
        part[s] = jnp.sum(jnp.abs(window[lax.rem(s, HELD)]), axis=0, keepdims=True)

    def scaled(s):
        slot, held = lax.rem(s, WINDOW), lax.rem(s, HELD)
        total = both[s]
        for i in range(len(alike)):
            total = total + others[s, i]
        scale = total / depth
        scales[s] = scale
        inverse = 1.0 / scale
        for at in range(0, width, 128):
            w = window[held, :, at : at + 128] * inverse[:, at : at + 128]
            stage[slot, at : at + 128, :] = w.T.astype(jnp.bfloat16)

    row_block[...] = (router[...] * gain[...]).astype(jnp.bfloat16)
    own = pltpu.make_async_copy(row_block, routed.at[me, mine], own_sem)
    along_z = [
        pltpu.make_async_remote_copy(
            row_block, routed.at[me, mine], z_send.at[i], z_recv.at[i],
            device_id=(c, me), device_id_type=MESH,
        )
        for i, c in enumerate(columns)
    ]
    along_rows = [
        pltpu.make_async_remote_copy(
            routed.at[me], routed.at[me], r_send.at[i], r_recv.at[i],
            device_id=(mine, p), device_id_type=MESH,
        )
        for i, p in enumerate(peers)
    ]

    for s in range(LOADS):
        load(jnp.int32(s), True)
    pl.semaphore_wait(barrier, len(peers) + len(columns))

    @pl.loop(0, units + LAG + 1)
    def _(i):
        @pl.when(i < units)
        def _():
            load(i, False)
            summed(i)

        @pl.when((i >= PAIR_LAG) & (i < units + PAIR_LAG))
        def _():
            s = i - PAIR_LAG
            pair(s).wait()
            both[s] = part[s] + partner[s]

        @pl.when((i >= LAG) & (i < units + LAG))
        def _():
            s = i - LAG

            @pl.when(s >= WINDOW)
            def _():
                settle(s - WINDOW)

            for copy in chips(s):
                copy.wait()
            scaled(s)

        @pl.when(i < units)
        def _():
            pair(i).start()

        @pl.when((i >= PAIR_LAG) & (i < units + PAIR_LAG))
        def _():
            for copy in chips(i - PAIR_LAG):
                copy.start()

        load(i + LOADS, True)

        @pl.when(i >= LAG + 1)
        def _():
            send(i - LAG - 1)

        @pl.when(i == LAG + 2)
        def _():
            own.start()
            for copy in along_z:
                copy.start()

        @pl.when(i == units // 2)
        def _():
            own.wait()
            for copy in along_z:
                copy.wait()
            for copy in along_rows:
                copy.start()

    @pl.loop(max(units - WINDOW, 0), units)
    def _(s):
        settle(s)

    for copy in along_rows:
        copy.wait()


def arrange(n, routed, gate_in, up_in, gate_out, up_out, router_out):
    rest = gate_in.shape[3]
    for source, target in ((gate_in, gate_out), (up_in, up_out)):
        for p in range(n):
            target[0, :, p * rest : (p + 1) * rest] = source[0, p]

    @pl.when(pl.program_id(0) == 0)
    def _():
        for p in range(n):
            block = routed[p].astype(jnp.float32).reshape(-1, rest)
            router_out[p * rest : (p + 1) * rest, :] = block.T.astype(jnp.bfloat16)


def in_kernels(n, owners, w_gate, w_up, router_weight, router_gain):
    experts, rows, width = w_gate.shape
    piece, units, across = width // n, 2 * experts, router_weight.shape[1]
    depth = n * rows
    anywhere, vmem = pl.BlockSpec(memory_space=pl.ANY), pl.BlockSpec(memory_space=pltpu.VMEM)
    dma = pltpu.SemaphoreType.DMA
    pieces, routed, scales = pl.pallas_call(
        functools.partial(exchange, experts, n, owners, float(depth)),
        out_shape=(
            jax.ShapeDtypeStruct((units, n, piece, rows), jnp.bfloat16),
            jax.ShapeDtypeStruct((n, owners, across, rows), jnp.bfloat16),
            jax.ShapeDtypeStruct((units, 1, width), jnp.float32),
        ),
        in_specs=[anywhere, anywhere, vmem, vmem],
        out_specs=(anywhere, anywhere, vmem),
        scratch_shapes=[
            pltpu.VMEM((HELD, rows, width), jnp.float32),
            pltpu.VMEM((WINDOW, width, rows), jnp.bfloat16),
            pltpu.VMEM((across, rows), jnp.bfloat16),
            pltpu.VMEM((units, 1, width), jnp.float32),
            pltpu.VMEM((units, 1, width), jnp.float32),
            pltpu.VMEM((units, 1, width), jnp.float32),
            pltpu.VMEM((units, n // 2 - 1, 1, width), jnp.float32),
            dma((HELD,)), dma((WINDOW, n - 1)), dma((2 * WINDOW, n - 1)), dma((WINDOW,)),
            dma((SUMS,)), dma((SUMS,)), dma((SUMS, n // 2 - 1)), dma((SUMS, n // 2 - 1)),
            dma, dma((owners,)), dma((owners,)), dma((n - 1,)), dma((n - 1,)),
        ],
        compiler_params=pltpu.CompilerParams(
            collective_id=0, has_side_effects=True, vmem_limit_bytes=32 * 2**20
        ),
        name="exchange",
    )(w_gate, w_up, router_weight.T, router_gain[None, :])
    own_scale = lax.dynamic_slice_in_dim(
        scales[:, 0, :], lax.axis_index("rows") * piece, piece, axis=1
    )

    full = lambda shape: pl.BlockSpec(shape, lambda e: (0,) * len(shape))
    gate, up, router = pl.pallas_call(
        functools.partial(arrange, n),
        grid=(experts,),
        out_shape=(
            jax.ShapeDtypeStruct((experts, piece, depth), jnp.bfloat16),
            jax.ShapeDtypeStruct((experts, piece, depth), jnp.bfloat16),
            jax.ShapeDtypeStruct((depth, owners * across), jnp.bfloat16),
        ),
        in_specs=[
            full(routed.shape),
            pl.BlockSpec((1, n, piece, rows), lambda e: (e, 0, 0, 0)),
            pl.BlockSpec((1, n, piece, rows), lambda e: (experts + e, 0, 0, 0)),
        ],
        out_specs=(
            pl.BlockSpec((1, piece, depth), lambda e: (e, 0, 0)),
            pl.BlockSpec((1, piece, depth), lambda e: (e, 0, 0)),
            full((depth, owners * across)),
        ),
        compiler_params=pltpu.CompilerParams(
            dimension_semantics=("arbitrary",), vmem_limit_bytes=32 * 2**20
        ),
        name="arrange",
    )(routed, pieces, pieces)
    return (
        jnp.swapaxes(gate, 1, 2), jnp.swapaxes(up, 1, 2),
        own_scale[:experts], own_scale[experts:], router,
    )


def in_ops(n, w_gate, w_up, router_weight, router_gain):
    depth = n * w_gate.shape[1]
    sums = (jnp.sum(jnp.abs(w_gate), axis=1), jnp.sum(jnp.abs(w_up), axis=1))
    served, scales = [], []
    for w, total in zip((w_gate, w_up), lax.psum(sums, "rows")):
        scale = total / depth
        narrow = (w / jnp.expand_dims(scale, 1)).astype(jnp.bfloat16)
        piece = lax.all_to_all(narrow, "rows", split_axis=2, concat_axis=1, tiled=True)
        size = piece.shape[2]
        served.append(piece)
        scales.append(lax.dynamic_slice_in_dim(scale, lax.axis_index("rows") * size, size, axis=1))
    part = (router_weight * router_gain[:, None]).astype(jnp.bfloat16)
    router = lax.all_gather(part, "rows", axis=0, tiled=True)
    router = lax.all_gather(router, "owner", axis=1, tiled=True)
    return (*served, *scales, router)


def solution(mesh):
    n, owners = mesh.shape["rows"], mesh.shape["owner"]

    def on_device(w_gate, w_up, router_weight, router_gain):
        experts, rows, width = w_gate.shape
        whole_tiles = (
            rows % 128 == 0 and width % (16 * n) == 0 and width % 128 == 0
            and n & (n - 1) == 0 and n > 2 and owners > 1
        )
        if whole_tiles:
            return in_kernels(n, owners, w_gate, w_up, router_weight, router_gain)
        return in_ops(n, w_gate, w_up, router_weight, router_gain)

    placed = (P("owner", "rows", None), P("owner", "rows", None), P("rows", "owner"), P("rows"))
    return jax.shard_map(
        on_device,
        mesh=mesh,
        in_specs=placed,
        out_specs=(
            P("owner", None, "rows"),
            P("owner", None, "rows"),
            P("owner", "rows"),
            P("owner", "rows"),
            P(),
        ),
        check_vma=False,
    )
```

time: 483 us -> 331 us (0.69)
  Pallas kernels: 0 us -> 326 us
  blocking collectives: 158 us -> 0 us
  waiting for transfers between devices: 131 us -> 0 us
  local copies, waits for them, and re-layouts: 120 us -> 2.19 us
  other arithmetic: 46.6 us -> 0 us
  between operations: 14.1 us -> 0.65 us
  starting transfers between devices: 10.8 us -> 0 us
    pallas_call x0 -> x2, Pallas kernels: none -> 326 us  [the longest x1 297 us: in_kernels(): pl.pallas_call(functools.partial(exchange, experts, n, owners, float(dept...]
    all_gather x2 -> x0, blocking collectives: 158 us -> none  [the longest x1 142 us: on_device(): row_router = lax.all_gather(part_router, 'rows', axis=0, tiled=True)]
    all_to_all x2 -> x0, waiting for transfers between devices: 99.5 us -> none  [the longest x1 99.5 us: on_device(): lax.all_to_all(narrow_up, 'rows', split_axis=2, concat_axis=1, tiled=True)]
    all_to_all x4 -> x0, local copies, waits for them, and re-layouts: 67.1 us -> none  [the longest x2 33.6 us: on_device(): lax.all_to_all(narrow_gate, 'rows', split_axis=2, concat_axis=1, tiled=True)]
    unnamed x9 -> x4, local copies, waits for them, and re-layouts: 51.3 us -> 1.43 us
    psum x1 -> x0, waiting for transfers between devices: 31.5 us -> none  [on_device(): lax.psum((jnp.sum(jnp.abs(w_gate), axis=1), jnp.sum(jnp.abs(w_up), axis=1...]
    convert_element_type x3 -> x0, other arithmetic: 28.3 us -> none  [the longest x1 14.1 us: on_device(): (w_gate / jnp.expand_dims(scale_gate, 1)).astype(jnp.bfloat16)]
    reduce_sum x1 -> x0, other arithmetic: 17.4 us -> none  [on_device(): jnp.sum(jnp.abs(w_up), axis=1)]
  transfers between devices with their start and end apart: 3 -> 0, of which waited for: 2 -> 0; matrix products, arithmetic and copies ran while one was open for 17% -> 0% of each run, Pallas kernels for 0% -> 0%
where the time goes in v1:
time: 331 us; the launch traced here: 329 us
  Pallas kernels  326 us (98%)
    pallas_call x1, Pallas kernels, in_kernels(): pl.pallas_call(functools.partial(exchange, experts, n, owners, float(dept...  297 us
    pallas_call x1, Pallas kernels, in_kernels(): pl.pallas_call(functools.partial(arrange, n), grid=(experts,), out_shape=...  29.9 us

profile of v1, /device:TPU:0, one launch (start us, length us, event | category | flops | bytes accessed | tf_op | source)
XLA Modules:
  0.0 329.3 jit_solution(12679928427336553430)
XLA Ops:
  0.6 0.0 copy-start
  0.6 0.7 copy-done
  1.4 0.0 copy-start.1
  1.4 0.7 copy-done.1
  2.1 296.5 %exchange.1 = (bf16[64,8,96,256]{3,2,1,0:T(8,128)(2,1)}, bf16[8,4,32,256]{3,2,1,0:T(8,128)(2,1)S(1)}, f32[64,1,768]{2,1,0:T(1,128)S(1)}) custom-call(f32[32,256,768]{2,1,0:T(8,128)} %gate.1, f32[32,256,768]{2,1,0:T(8,128)} %up.1, f32[32,256]{1,0:T(8,128)S(1)} %bitcast.6, f32[1,256]{1,0:T(1,128)S(1)} %bitcast.7), custom_call_target="tpu_custom_call" | custom-call | tf_op jit(solution)/shard_map/exchange/pallas_call | solution.py:222
  298.6 0.8 constant_dynamic-slice_fusion.1
  299.4 29.9 %arrange.1 = (bf16[32,96,2048]{2,1,0:T(8,128)(2,1)}, bf16[32,96,2048]{2,1,0:T(8,128)(2,1)}, bf16[2048,128]{1,0:T(8,128)(2,1)}) custom-call(bf16[8,4,32,256]{3,2,1,0:T(8,128)(2,1)S(1)} %get-tuple-element.11.routed, bf16[64,8,96,256]{3,2,1,0:T(8,128)(2,1)} %get-tuple-element.12.gate_in.up_in, bf16[64,8,96,256]{3,2,1,0:T(8,128)(2,1)} %get-tuple-element.12.gate_in.up_in), custom_call_target="tpu_custom_call" | custom-call | tf_op jit(solution)/shard_map/arrange/pallas_call | solution.py:253
Async XLA Ops:
  0.6 0.8 copy-start
  1.4 0.7 copy-start.1
